TPU v7x, 256 devices: a whole 4x4x8 slice. The times are simulated.
256 devices in a mesh: section: 16 (over z_lo, y, core), dp: 16 (over z_hi, x).
Axes of the slice: x: 4, y: 4, z: 8 (z_hi: 4, z_lo: 2; z = z_hi * 2 + z_lo), core: 2. Of those that a mesh axis runs over, the one named last changes fastest.
Arguments:
- w_in: bfloat16 [16, 5120, 4096], P('section', 'dp'), may hold values from -0.09375 to 0.09375
- w_out: bfloat16 [16, 5120, 4096], P('section', 'dp'), may hold values from -0.078125 to 0.078125
- input_stash: bfloat16 [16, 2, 128, 4096], P('section', None, 'dp'), may hold values from -6 to 6
- hidden_stash: bfloat16 [16, 2, 128, 5120], P('section', None, None, 'dp'), may hold values from -6 to 6
- gate_stash: float32 [16, 2, 128], P('section'), may hold values from 0.25 to 1
- block_pick: int32 [16, 2], P('section'), may hold values from 0 to 1
- slot_order: int32 [16, 2], P('section'), may hold values from 0 to 1, each once within a row
- arriving: bfloat16 [16, 2, 128, 4096], P('section', None, 'dp'), may hold values from -6 to 6
- loss_grads: bfloat16 [1, 2, 128, 4096], P(None, None, 'dp'), may hold values from -6 to 6
Outputs:
- passed: bfloat16 [16, 2, 2, 128, 4096], P('section', None, None, 'dp')
- grad_in: bfloat16 [16, 5120, 4096], P('section', 'dp')
- grad_out: bfloat16 [16, 5120, 4096], P('section', 'dp')
- gate_grads: float32 [16, 2, 128], P('section')
Inputs may be any that keep to these rules, and one draw needn't show every extreme that they name: Each row of slot_order holds every slot 0 to 1 once.
All inputs are finite; a program needn't handle non-finite values.
Results may differ from a plain program's by a relative error of at most 0.0055.
Values may be sent and summed in bfloat16 or wider, within the bound.
A program may use at most 128 MiB of HBM per device.

v0:
```python
import jax
import jax.numpy as jnp
from jax import lax
from jax.sharding import PartitionSpec as P


def shifted_2(block, axis, distance):
    devices = range(lax.axis_size(axis))
    route = [(i - distance, i) for i in devices if i - distance in devices]
    return lax.ppermute(block, axis, route)


def per_device(
    w_in, w_out, input_stash, hidden_stash, gate_stash, block_pick, slot_order, arriving, loss_grads
):
    in_weight = w_in[0]
    out_weight = w_out[0]
    ticks = slot_order.shape[1]
    blocks = arriving.shape[1]
    is_top = lax.axis_index("section") == lax.axis_size("section") - 1
    contract = (((0,), (0,)), ((), ()))

    def section_tick(incoming, tick_index):
        slot_id = slot_order[0, tick_index]
        block_id = block_pick[0, slot_id]
        gate_vals = gate_stash[0, slot_id]
        pre_act = hidden_stash[0, slot_id]
        own_rows = incoming[block_id]
        rows_input, rows_grad = (
            lax.all_gather(input_stash[0, slot_id], "dp", axis=0, tiled=True),
            lax.all_gather(own_rows, "dp", axis=0, tiled=True),
        )
        upstream = lax.dot_general(
            rows_grad, out_weight, (((1,), (1,)), ((), ())), preferred_element_type=jnp.float32
        )
        active = jnp.maximum(pre_act.astype(jnp.float32), 0.0)
        hid_grad = jnp.where(pre_act > 0, upstream * gate_vals[:, None], 0.0).astype(jnp.bfloat16)
        input_part = lax.psum_scatter(
            jnp.dot(hid_grad, in_weight, preferred_element_type=jnp.float32),
            "dp",
            scatter_dimension=0,
            tiled=True,
        )
        placed = jnp.where((jnp.arange(blocks) == block_id)[:, None, None], input_part[None], 0.0)
        updated = (incoming.astype(jnp.float32) + placed).astype(jnp.bfloat16)
        gate_part = jnp.sum(active * upstream, axis=1)
        gate_part = lax.psum(gate_part, "dp")
        weighted = (active * gate_vals[:, None]).astype(jnp.bfloat16)
        return (updated, gate_part, (rows_grad, weighted, hid_grad, rows_input))

    def weight_terms(pieces):
        rows_grad, weighted, hid_grad, rows_input = pieces
        out_term = lax.dot_general(
            weighted, rows_grad, contract, preferred_element_type=jnp.float32
        )
        in_term = lax.dot_general(
            hid_grad, rows_input, contract, preferred_element_type=jnp.float32
        )
        return (out_term, in_term)

    start_sums = (jnp.zeros(out_weight.shape, jnp.float32), jnp.zeros(in_weight.shape, jnp.float32))

    def advance(carry, extra):
        incoming, sums = carry
        tick_index, loss_rows = extra
        updated, gate_part, pieces = section_tick(incoming, tick_index)
        terms = weight_terms(pieces)
        sums = (sums[0] + terms[0], sums[1] + terms[1])
        shifted = shifted_2(updated, "section", -1)
        following = jnp.where(is_top, loss_rows, shifted)
        return ((following, sums), (updated, gate_part))

    (last_in, sums), (early_out, early_gate) = lax.scan(
        advance, (arriving[0], start_sums), (jnp.arange(ticks - 1), loss_grads)
    )
    last_out, last_gate, last_pieces = section_tick(last_in, ticks - 1)
    terms = weight_terms(last_pieces)
    out_sum = sums[0] + terms[0]
    in_sum = sums[1] + terms[1]
    passed = jnp.concatenate([early_out, last_out[None]], axis=0)
    gate_parts = jnp.concatenate([early_gate, last_gate[None]], axis=0)
    onehot = (slot_order[0][:, None] == jnp.arange(ticks)[None, :]).astype(jnp.float32)
    gate_grads = jnp.einsum("tp,tr->pr", onehot, gate_parts, precision=lax.Precision.HIGHEST)
    return (
        passed[None],
        in_sum.astype(jnp.bfloat16)[None],
        out_sum.astype(jnp.bfloat16)[None],
        gate_grads[None],
    )


def solution(mesh):
    placed = (
        P("section", "dp", None),
        P("section", "dp", None),
        P("section", None, "dp", None),
        P("section", None, None, "dp"),
        P("section", None, None),
        P("section", None),
        P("section", None),
        P("section", None, "dp", None),
        P(None, None, "dp", None),
    )
    return jax.shard_map(
        per_device,
        mesh=mesh,
        in_specs=placed,
        out_specs=(
            P("section", None, None, "dp", None),
            P("section", "dp", None),
            P("section", "dp", None),
            P("section", None, None),
        ),
        check_vma=False,
    )
```

profile of v0, /device:TPU:8, one launch (start us, length us, event | category | flops | bytes accessed | tf_op | source)
XLA Modules:
  0.0 431.0 jit_solution(4442010572938618943)
XLA Ops:
  7.2 1.4 fusion.47
  12.5 1.3 constant_dynamic-slice_fusion.4
  15.8 1.5 constant_dynamic-slice_fusion.6
  17.3 0.8 fusion.42
  18.1 56.0 %all-gather.9.cloned.1.call-done = bf16[1,1,128,4096]{3,2,1,0:T(8,128)(2,1)} async-done(((bf16[1,1,8,4096]{3,2,1,0:T(8,128)(2,1)}), bf16[1,1,128,4096]{3,2,1,0:T(8,128)(2,1)}) %all-gather.9.cloned.1.call-update) | async-done | bytes 1048592 | tf_op jit(solution)/shard_map/while/body/eval_jaxpr/all_gather | solution.py:31
  74.1 2.9 select_convert_fusion.1
  77.0 2.1 fusion.6
  79.1 0.7 iota_compare_fusion.1
  79.8 85.0 %reduce-scatter.3.cloned.1.call-done = f32[8,4096]{1,0:T(8,128)} async-done(((f32[128,4096]{1,0:T(8,128)}), f32[8,4096]{1,0:T(8,128)}) %reduce-scatter.3.cloned.1.call-update) | async-done | bytes 131088 | tf_op jit(solution)/shard_map/while/body/eval_jaxpr/reduce_scatter | solution.py:38
  164.7 1.0 fusion.22
  165.7 1.9 collective-permute-start
  169.6 0.6 collective-permute-done
  170.2 0.9 bitcast_select_fusion
  171.1 0.6 constant_dynamic-slice_fusion.3
  171.8 1.5 constant_dynamic-slice_fusion
  173.4 0.5 all-gather.15.cloned.1.call-update
  174.0 51.0 %all-gather.11.cloned.1.call-done = bf16[1,128,4096]{2,1,0:T(8,128)(2,1)} async-done(((bf16[1,8,4096]{2,1,0:T(8,128)(2,1)}), bf16[1,128,4096]{2,1,0:T(8,128)(2,1)}) %all-gather.11.cloned.1.call-update) | async-done | bytes 1048592 | tf_op jit(solution)/shard_map/all_gather | solution.py:31
  225.0 2.9 fusion.26
  227.9 2.1 fusion.4
  230.0 0.7 iota_compare_fusion
  230.7 4.4 %fusion.17 = f32[320,4096]{1,0:T(8,128)} fusion(bf16[1,1,128,4096]{3,2,1,0:T(8,128)(2,1)} %all-gather.9.cloned.1.call-done, f32[128]{0:T(128)S(1)} %get-tuple-element.42, bf16[1,2,128,320]{2,3,1,0:T(8,128)(2,1)S(1)} %copy-done.1, s32[]{:T(128)S(6)} %select_n.57), kind=kOutput, calls=%fused_computation.20 | convolution fusion | flops 335708160 | bytes 6373892 | tf_op jit(solution)/shard_map/while/body/eval_jaxpr/dot_general | solution.py:53
  235.1 43.8 %all-gather.13.cloned.1.call-done = bf16[1,1,128,4096]{3,2,1,0:T(8,128)(2,1)} async-done(((bf16[1,1,8,4096]{3,2,1,0:T(8,128)(2,1)}), bf16[1,1,128,4096]{3,2,1,0:T(8,128)(2,1)}) %all-gather.13.cloned.1.call-update) | async-done | bytes 1048592 | tf_op jit(solution)/shard_map/while/body/eval_jaxpr/all_gather | solution.py:30
  278.9 4.4 %fusion.13 = f32[320,4096]{1,0:T(8,128)} fusion(bf16[128,320]{0,1:T(8,128)(2,1)S(1)} %get-tuple-element.62, bf16[1,1,128,4096]{3,2,1,0:T(8,128)(2,1)} %all-gather.13.cloned.1.call-done), kind=kOutput, calls=%fused_computation.16 | convolution fusion | flops 335544320 | bytes 6373376 | tf_op jit(solution)/shard_map/while/body/eval_jaxpr/dot_general | solution.py:56
  283.3 0.1 fusion.20
  283.4 42.8 %all-reduce = (f32[1,128]{1,0:T(1,128)S(1)}, f32[1,128]{1,0:T(1,128)S(1)}) all-reduce(f32[1,128]{1,0:T(1,128)S(1)} %bitcast.89, f32[1,128]{1,0:T(1,128)S(1)} %bitcast.88), channel_id=1, replica_groups=mesh['section'=16,'dp'=16] {'dp'}, use_global_device_ids=true, to_apply=%region_5.6 | all-reduce | flops 256 | bytes 2048 | tf_op jit(solution)/shard_map/psum | solution.py:47
  326.2 0.8 convolution_bitcast_fusion
  327.0 5.2 %fusion.2 = bf16[1,320,4096]{2,1,0:T(8,128)(2,1)} fusion(f32[320,4096]{1,0:T(8,128)} %fusion.17, bf16[1,128,4096]{2,1,0:T(8,128)(2,1)} %all-gather.11.cloned.1.call-done, f32[128]{0:T(128)S(1)} %get-tuple-element.41, bf16[1,2,128,320]{2,3,1,0:T(8,128)(2,1)S(1)} %copy-done.1, s32[]{:T(128)S(6)} %select_n.64), kind=kOutput, calls=%fused_computation.4 | convolution fusion | flops 338329600 | bytes 8995332 | tf_op jit(solution)/shard_map/dot_general | solution.py:53
  332.1 0.2 all-gather.15.cloned.1.call-done
  332.3 5.1 %fusion.3 = bf16[1,320,4096]{2,1,0:T(8,128)(2,1)} fusion(f32[320,4096]{1,0:T(8,128)} %fusion.13, bf16[128,320]{0,1:T(8,128)(2,1)S(1)} %get-tuple-element.38, bf16[1,1,128,4096]{3,2,1,0:T(8,128)(2,1)} %all-gather.15.cloned.1.call-done), kind=kOutput, calls=%fused_computation.5 | convolution fusion | flops 338165760 | bytes 8994816 | tf_op jit(solution)/shard_map/dot_general | solution.py:56
  337.4 84.9 %reduce-scatter.5.cloned.1.call-done = f32[8,4096]{1,0:T(8,128)} async-done(((f32[128,4096]{1,0:T(8,128)}), f32[8,4096]{1,0:T(8,128)}) %reduce-scatter.5.cloned.1.call-update) | async-done | bytes 131088 | tf_op jit(solution)/shard_map/reduce_scatter | solution.py:38
  422.4 1.0 fusion.27
  423.4 0.7 maximum_bitcast_fusion
  (23 shorter events, 0.4 us)
Async XLA Ops:
  7.2 69.8 %copy-start = (bf16[1,320,4096]{2,1,0:T(8,128)(2,1)S(1)}, bf16[1,320,4096]{2,1,0:T(8,128)(2,1)}, u32[]{:S(2)}) copy-start(bf16[1,320,4096]{2,1,0:T(8,128)(2,1)} %param.9) | copy-start | bytes 7864324
  7.2 66.9 %all-gather.9.cloned.1.call-start = ((), (), s32[]{:S(2)}) async-start(), calls=%async_computation.4 | async-start | bytes 1114112 | tf_op jit(solution)/shard_map/while/body/eval_jaxpr/all_gather | solution.py:31
  17.3 147.5 %reduce-scatter.3.cloned.1.call-start = ((), (), s32[]{:S(2)}) async-start(), calls=%async_computation.2 | async-start | bytes 2228224 | tf_op jit(solution)/shard_map/while/body/eval_jaxpr/reduce_scatter | solution.py:38
  76.9 87.8 %copy-start.2 = (bf16[1,2,8,4096]{3,2,1,0:T(8,128)(2,1)S(1)}, bf16[1,2,8,4096]{3,2,1,0:T(8,128)(2,1)}, u32[]{:S(2)}) copy-start(bf16[1,2,8,4096]{3,2,1,0:T(8,128)(2,1)} %param.16) | copy-start | bytes 393220
  77.0 93.2 %copy-start.4 = (bf16[1,2,8,4096]{3,2,1,0:T(8,128)(2,1)S(1)}, bf16[1,2,8,4096]{3,2,1,0:T(8,128)(2,1)}, u32[]{:S(2)}) copy-start(bf16[1,2,8,4096]{3,2,1,0:T(8,128)(2,1)} %param.17) | copy-start | bytes 393220
  79.0 145.9 %copy-start.1 = (bf16[1,2,128,320]{2,3,1,0:T(8,128)(2,1)S(1)}, bf16[1,2,128,320]{2,3,1,0:T(8,128)(2,1)}, u32[]{:S(2)}) copy-start(bf16[1,2,128,320]{2,3,1,0:T(8,128)(2,1)} %param.12) | copy-start | bytes 491524
  79.1 145.9 %all-gather.11.cloned.1.call-start = ((), (), s32[]{:S(2)}) async-start(), calls=%async_computation.5 | async-start | bytes 1114112 | tf_op jit(solution)/shard_map/all_gather | solution.py:31
  165.7 4.4 %collective-permute-start = (bf16[2,8,4096]{2,1,0:T(8,128)(2,1)S(1)}, bf16[2,8,4096]{2,1,0:T(8,128)(2,1)}, u32[]{:S(2)}, u32[]{:S(2)}) collective-permute-start(bf16[2,8,4096]{2,1,0:T(8,128)(2,1)S(1)} %fusion.22), channel_id=1, source_target_pairs={{16,0},{32,16},{48,32},{64,48},{80,64},{96,80},{112,96},{128,112},... | collective-permute-start | bytes 393224 | tf_op jit(solution)/shard_map/while/body/eval_jaxpr/ppermute | solution.py:10
  171.8 107.1 %all-gather.13.cloned.1.call-start = ((), (), s32[]{:S(2)}) async-start(), calls=%async_computation.6 | async-start | bytes 1114112 | tf_op jit(solution)/shard_map/while/body/eval_jaxpr/all_gather | solution.py:30
  173.4 158.9 %all-gather.15.cloned.1.call-start = ((), (), s32[]{:S(2)}) async-start(), calls=%async_computation.7 | async-start | bytes 1114112 | tf_op jit(solution)/shard_map/all_gather | solution.py:30
  174.0 248.4 %reduce-scatter.5.cloned.1.call-start = ((), (), s32[]{:S(2)}) async-start(), calls=%async_computation.3 | async-start | bytes 2228224 | tf_op jit(solution)/shard_map/reduce_scatter | solution.py:38
  235.1 48.2 %copy-start.3 = (f32[8,4096]{1,0:T(8,128)S(1)}, f32[8,4096]{1,0:T(8,128)}, u32[]{:S(2)}) copy-start(f32[8,4096]{1,0:T(8,128)} %reduce-scatter.3.cloned.1.call-done) | copy-start | bytes 393220
  235.1 91.1 %copy-start.5 = (s32[1,2]{1,0:T(1,128)S(1)}, s32[1,2]{1,0:T(1,128)}, u32[]{:S(2)}) copy-start(s32[1,2]{1,0:T(1,128)} %param.15) | copy-start | bytes 28
Sparse Core Ops, SparseCore 0:
  17.4 56.6 all-gather.8
  79.2 85.5 reduce-scatter.2
  171.9 53.0 all-gather.10
  228.1 50.7 all-gather.12
  282.1 50.1 all-gather.14
  336.1 86.1 reduce-scatter.4
where the time goes:
time: 432 us; the launch traced here: 431 us
  waiting for transfers between devices  322 us (75%)
  blocking collectives  42.8 us (10%)
  matrix products  29.8 us (7%)
  between operations  22 us (5%)
  local copies, waits for them, and re-layouts  7.18 us (2%)
  other arithmetic  5.06 us (1%)
    reduce_scatter x2, waiting for transfers between devices, section_tick(): lax.psum_scatter(jnp.dot(hid_grad, in_weight, preferred_element_type=jnp....  170 us
    all_gather x2, waiting for transfers between devices, section_tick(): lax.all_gather(own_rows, 'dp', axis=0, tiled=True)  107 us
    all_gather x2, waiting for transfers between devices, section_tick(): lax.all_gather(input_stash[0, slot_id], 'dp', axis=0, tiled=True)  44 us
    psum x1, blocking collectives, section_tick(): gate_part = lax.psum(gate_part, 'dp')  42.8 us
    dot_general x2, matrix products, weight_terms(): lax.dot_general(weighted, rows_grad, contract, preferred_element_type=jnp...  9.57 us
    dot_general x2, matrix products, weight_terms(): lax.dot_general(hid_grad, rows_input, contract, preferred_element_type=jn...  9.5 us
  transfers between devices with their start and end apart: 7, of which 7 were waited for; matrix products, arithmetic and copies ran while one was open for 7% of the time, Pallas kernels for 0%

commit v1 on v0

--- a/solution.py
+++ b/solution.py
@@ -2,6 +2,7 @@
 import jax.numpy as jnp
 from jax import lax
 from jax.sharding import PartitionSpec as P
+from jax.lax import all_to_all, psum
 
 
 def shifted_2(block, axis, distance):
@@ -26,8 +27,11 @@
         gate_vals = gate_stash[0, slot_id]
         pre_act = hidden_stash[0, slot_id]
         own_rows = incoming[block_id]
+        squares_track = lambda m: jnp.concatenate(
+            all_to_all(jnp.stack([m] * psum(1, "dp")), "dp", 0, 0), axis=0
+        )
         rows_input, rows_grad = (
-            lax.all_gather(input_stash[0, slot_id], "dp", axis=0, tiled=True),
+            squares_track(input_stash[0, slot_id]),
             lax.all_gather(own_rows, "dp", axis=0, tiled=True),
         )
         upstream = lax.dot_general(

time: 432 us -> 355 us (0.82)
  waiting for transfers between devices: 322 us -> 222 us
  blocking collectives: 42.8 us -> 54.6 us
  starting transfers between devices: 2.17 us -> 12.6 us
    reduce_scatter x2, waiting for transfers between devices: 170 us -> 106 us  [section_tick(): lax.psum_scatter(jnp.dot(hid_grad, in_weight, preferred_element_type=jnp....]
    all_gather x2 -> x0, waiting for transfers between devices: 44 us -> none  [section_tick(): lax.all_gather(input_stash[0, slot_id], 'dp', axis=0, tiled=True)]
    psum x1, blocking collectives: 42.8 us -> 54.6 us  [section_tick(): gate_part = lax.psum(gate_part, 'dp')]
    all_to_all x0 -> x2, starting transfers between devices: none -> 10.5 us  [section_tick(): all_to_all(jnp.stack([m] * psum(1, 'dp')), 'dp', 0, 0)]
    all_gather x2, waiting for transfers between devices: 107 us -> 115 us  [section_tick(): lax.all_gather(own_rows, 'dp', axis=0, tiled=True)]
  transfers between devices with their start and end apart: 7 -> 7, of which waited for: 7 -> 5; matrix products, arithmetic and copies ran while one was open for 7% -> 9% of each run, Pallas kernels for 0% -> 0%
where the time goes in v1:
time: 355 us; the launch traced here: 354 us
  waiting for transfers between devices  222 us (63%)
  blocking collectives  54.6 us (15%)
  matrix products  29.9 us (8%)
  between operations  21.7 us (6%)
  starting transfers between devices  12.6 us (4%)
  local copies, waits for them, and re-layouts  8.68 us (2%)
  other arithmetic  5.09 us (1%)
    all_gather x2, waiting for transfers between devices, section_tick(): lax.all_gather(own_rows, 'dp', axis=0, tiled=True)  115 us
    reduce_scatter x2, waiting for transfers between devices, section_tick(): lax.psum_scatter(jnp.dot(hid_grad, in_weight, preferred_element_type=jnp....  106 us
    psum x1, blocking collectives, section_tick(): gate_part = lax.psum(gate_part, 'dp')  54.6 us
    all_to_all x2, starting transfers between devices, section_tick(): all_to_all(jnp.stack([m] * psum(1, 'dp')), 'dp', 0, 0)  10.5 us
    dot_general x2, matrix products, weight_terms(): lax.dot_general(weighted, rows_grad, contract, preferred_element_type=jnp...  9.58 us
    dot_general x2, matrix products, weight_terms(): lax.dot_general(hid_grad, rows_input, contract, preferred_element_type=jn...  9.54 us
  transfers between devices with their start and end apart: 7, of which 5 were waited for; matrix products, arithmetic and copies ran while one was open for 9% of the time, Pallas kernels for 0%

profile of v1, /device:TPU:8, one launch (start us, length us, event | category | flops | bytes accessed | tf_op | source)
XLA Modules:
  0.0 354.2 jit_solution(11251658214536828007)
XLA Ops:
  7.2 1.4 fusion.47
  12.5 1.3 constant_dynamic-slice_fusion.2
  15.8 1.5 constant_dynamic-slice_fusion.4
  17.3 0.8 fusion.42
  18.1 56.0 %all-gather.5.cloned.1.call-done = bf16[1,1,128,4096]{3,2,1,0:T(8,128)(2,1)} async-done(((bf16[1,1,8,4096]{3,2,1,0:T(8,128)(2,1)}), bf16[1,1,128,4096]{3,2,1,0:T(8,128)(2,1)}) %all-gather.5.cloned.1.call-update) | async-done | bytes 1048592 | tf_op jit(solution)/shard_map/while/body/eval_jaxpr/all_gather | solution.py:35
  74.1 2.9 select_convert_fusion.1
  77.0 2.1 fusion.6
  79.1 0.7 iota_compare_fusion.1
  79.8 84.9 %reduce-scatter.3.cloned.1.call-done = f32[8,4096]{1,0:T(8,128)} async-done(((f32[128,4096]{1,0:T(8,128)}), f32[8,4096]{1,0:T(8,128)}) %reduce-scatter.3.cloned.1.call-update) | async-done | bytes 131088 | tf_op jit(solution)/shard_map/while/body/eval_jaxpr/reduce_scatter | solution.py:42
  164.7 1.0 fusion.22
  165.7 1.9 collective-permute-start
  169.6 0.6 collective-permute-done
  170.2 0.9 bitcast_select_fusion
  171.1 0.6 constant_dynamic-slice_fusion.1
  171.8 0.9 dynamic-slice_bitcast_fusion
  172.7 1.1 stack.7
  173.7 5.4 %all-to-all-start = ((bf16[16,8,4096]{2,1,0:T(8,128)(2,1)}), bf16[16,8,4096]{2,1,0:T(8,128)(2,1)}, u32[]{:S(2)}, u32[]{:S(2)}) async-start(bf16[16,8,4096]{2,1,0:T(8,128)(2,1)} %stack.7), calls=%async_computation.2 | async-start | bytes 2097152 | tf_op jit(solution)/shard_map/while/body/eval_jaxpr/all_to_all | solution.py:31
  179.2 58.8 %all-gather.7.cloned.1.call-done = bf16[1,128,4096]{2,1,0:T(8,128)(2,1)} async-done(((bf16[1,8,4096]{2,1,0:T(8,128)(2,1)}), bf16[1,128,4096]{2,1,0:T(8,128)(2,1)}) %all-gather.7.cloned.1.call-update) | async-done | bytes 1048592 | tf_op jit(solution)/shard_map/all_gather | solution.py:35
  238.0 2.9 fusion.26
  240.9 2.1 fusion.4
  243.0 0.7 iota_compare_fusion
  243.7 1.1 stack.8
  244.8 5.1 %all-to-all-start.1 = ((bf16[16,8,4096]{2,1,0:T(8,128)(2,1)}), bf16[16,8,4096]{2,1,0:T(8,128)(2,1)}, u32[]{:S(2)}, u32[]{:S(2)}) async-start(bf16[16,8,4096]{2,1,0:T(8,128)(2,1)} %stack.8), calls=%async_computation.3 | async-start | bytes 2097152 | tf_op jit(solution)/shard_map/all_to_all | solution.py:31
  249.9 4.4 %fusion.17 = f32[320,4096]{1,0:T(8,128)} fusion(bf16[1,1,128,4096]{3,2,1,0:T(8,128)(2,1)} %all-gather.5.cloned.1.call-done, f32[128]{0:T(128)S(1)} %get-tuple-element.42, bf16[1,2,128,320]{2,3,1,0:T(8,128)(2,1)S(1)} %copy-done.1, s32[]{:T(128)S(6)} %select_n.57), kind=kOutput, calls=%fused_computation.20 | convolution fusion | flops 335708160 | bytes 6373892 | tf_op jit(solution)/shard_map/while/body/eval_jaxpr/dot_general | solution.py:57
  254.3 4.4 %fusion.13 = f32[320,4096]{1,0:T(8,128)} fusion(bf16[128,320]{0,1:T(8,128)(2,1)S(1)} %get-tuple-element.62, bf16[16,8,4096]{2,1,0:T(8,128)(2,1)} %all-to-all-done), kind=kOutput, calls=%fused_computation.16 | convolution fusion | flops 335544320 | bytes 6373376 | tf_op jit(solution)/shard_map/while/body/eval_jaxpr/dot_general | solution.py:60
  258.8 54.6 %all-reduce = (f32[1,128]{1,0:T(1,128)S(1)}, f32[1,128]{1,0:T(1,128)S(1)}) all-reduce(f32[1,128]{1,0:T(1,128)S(1)} %bitcast.93, f32[1,128]{1,0:T(1,128)S(1)} %bitcast.92), channel_id=1, replica_groups=mesh['section'=16,'dp'=16] {'dp'}, use_global_device_ids=true, to_apply=%region_5.6 | all-reduce | flops 256 | bytes 2048 | tf_op jit(solution)/shard_map/psum | solution.py:51
  313.4 0.8 convolution_bitcast_fusion
  314.2 5.2 %fusion.2 = bf16[1,320,4096]{2,1,0:T(8,128)(2,1)} fusion(f32[320,4096]{1,0:T(8,128)} %fusion.17, bf16[1,128,4096]{2,1,0:T(8,128)(2,1)} %all-gather.7.cloned.1.call-done, f32[128]{0:T(128)S(1)} %get-tuple-element.41, bf16[1,2,128,320]{2,3,1,0:T(8,128)(2,1)S(1)} %copy-done.1, s32[]{:T(128)S(6)} %select_n.64), kind=kOutput, calls=%fused_computation.4 | convolution fusion | flops 338329600 | bytes 8995332 | tf_op jit(solution)/shard_map/dot_general | solution.py:57
  319.4 5.1 %fusion.3 = bf16[1,320,4096]{2,1,0:T(8,128)(2,1)} fusion(f32[320,4096]{1,0:T(8,128)} %fusion.13, bf16[128,320]{0,1:T(8,128)(2,1)S(1)} %get-tuple-element.38, bf16[16,8,4096]{2,1,0:T(8,128)(2,1)} %all-to-all-done.1), kind=kOutput, calls=%fused_computation.5 | convolution fusion | flops 338165760 | bytes 8994816 | tf_op jit(solution)/shard_map/dot_general | solution.py:60
  324.6 21.3 %reduce-scatter.5.cloned.1.call-done = f32[8,4096]{1,0:T(8,128)} async-done(((f32[128,4096]{1,0:T(8,128)}), f32[8,4096]{1,0:T(8,128)}) %reduce-scatter.5.cloned.1.call-update) | async-done | bytes 131088 | tf_op jit(solution)/shard_map/reduce_scatter | solution.py:42
  345.9 1.0 fusion.27
  346.9 0.7 maximum_bitcast_fusion
  (23 shorter events, 0.4 us)
Async XLA Ops:
  7.2 69.8 %copy-start = (bf16[1,320,4096]{2,1,0:T(8,128)(2,1)S(1)}, bf16[1,320,4096]{2,1,0:T(8,128)(2,1)}, u32[]{:S(2)}) copy-start(bf16[1,320,4096]{2,1,0:T(8,128)(2,1)} %param.9) | copy-start | bytes 7864324
  7.2 66.9 %all-gather.5.cloned.1.call-start = ((), (), s32[]{:S(2)}) async-start(), calls=%async_computation.6 | async-start | bytes 1114112 | tf_op jit(solution)/shard_map/while/body/eval_jaxpr/all_gather | solution.py:35
  17.3 147.5 %reduce-scatter.3.cloned.1.call-start = ((), (), s32[]{:S(2)}) async-start(), calls=%async_computation.4 | async-start | bytes 2228224 | tf_op jit(solution)/shard_map/while/body/eval_jaxpr/reduce_scatter | solution.py:42
  76.9 87.8 %copy-start.2 = (bf16[1,2,8,4096]{3,2,1,0:T(8,128)(2,1)S(1)}, bf16[1,2,8,4096]{3,2,1,0:T(8,128)(2,1)}, u32[]{:S(2)}) copy-start(bf16[1,2,8,4096]{3,2,1,0:T(8,128)(2,1)} %param.16) | copy-start | bytes 393220
  77.0 93.2 %copy-start.4 = (bf16[1,2,8,4096]{3,2,1,0:T(8,128)(2,1)S(1)}, bf16[1,2,8,4096]{3,2,1,0:T(8,128)(2,1)}, u32[]{:S(2)}) copy-start(bf16[1,2,8,4096]{3,2,1,0:T(8,128)(2,1)} %param.17) | copy-start | bytes 393220
  79.1 158.9 %copy-start.1 = (bf16[1,2,128,320]{2,3,1,0:T(8,128)(2,1)S(1)}, bf16[1,2,128,320]{2,3,1,0:T(8,128)(2,1)}, u32[]{:S(2)}) copy-start(bf16[1,2,128,320]{2,3,1,0:T(8,128)(2,1)} %param.12) | copy-start | bytes 491524
  79.1 158.9 %all-gather.7.cloned.1.call-start = ((), (), s32[]{:S(2)}) async-start(), calls=%async_computation.7 | async-start | bytes 1114112 | tf_op jit(solution)/shard_map/all_gather | solution.py:35
  165.7 4.4 %collective-permute-start = (bf16[2,8,4096]{2,1,0:T(8,128)(2,1)S(1)}, bf16[2,8,4096]{2,1,0:T(8,128)(2,1)}, u32[]{:S(2)}, u32[]{:S(2)}) collective-permute-start(bf16[2,8,4096]{2,1,0:T(8,128)(2,1)S(1)} %fusion.22), channel_id=1, source_target_pairs={{16,0},{32,16},{48,32},{64,48},{80,64},{96,80},{112,96},{128,112},... | collective-permute-start | bytes 393224 | tf_op jit(solution)/shard_map/while/body/eval_jaxpr/ppermute | solution.py:11
  173.7 69.9 %all-to-all-start = ((bf16[16,8,4096]{2,1,0:T(8,128)(2,1)}), bf16[16,8,4096]{2,1,0:T(8,128)(2,1)}, u32[]{:S(2)}, u32[]{:S(2)}) async-start(bf16[16,8,4096]{2,1,0:T(8,128)(2,1)} %stack.7), calls=%async_computation.2 | async-start | bytes 2097152 | tf_op jit(solution)/shard_map/while/body/eval_jaxpr/all_to_all | solution.py:31
  179.2 166.7 %reduce-scatter.5.cloned.1.call-start = ((), (), s32[]{:S(2)}) async-start(), calls=%async_computation.5 | async-start | bytes 2228224 | tf_op jit(solution)/shard_map/reduce_scatter | solution.py:42
  244.8 74.7 %all-to-all-start.1 = ((bf16[16,8,4096]{2,1,0:T(8,128)(2,1)}), bf16[16,8,4096]{2,1,0:T(8,128)(2,1)}, u32[]{:S(2)}, u32[]{:S(2)}) async-start(bf16[16,8,4096]{2,1,0:T(8,128)(2,1)} %stack.8), calls=%async_computation.3 | async-start | bytes 2097152 | tf_op jit(solution)/shard_map/all_to_all | solution.py:31
  254.3 4.4 %copy-start.3 = (f32[8,4096]{1,0:T(8,128)S(1)}, f32[8,4096]{1,0:T(8,128)}, u32[]{:S(2)}) copy-start(f32[8,4096]{1,0:T(8,128)} %reduce-scatter.3.cloned.1.call-done) | copy-start | bytes 393220
  254.3 59.1 %copy-start.5 = (s32[1,2]{1,0:T(1,128)S(1)}, s32[1,2]{1,0:T(1,128)}, u32[]{:S(2)}) copy-start(s32[1,2]{1,0:T(1,128)} %param.15) | copy-start | bytes 28
Sparse Core Ops, SparseCore 0:
  17.4 56.6 all-gather.4
  79.2 85.5 reduce-scatter.2
  171.9 66.0 all-gather.6
  243.1 102.7 reduce-scatter.4
